TPU v7x, 32 devices: a whole 2x2x4 slice. The times are simulated.
32 devices in a mesh: lat: 8 (over y, x, core), lon: 4 (over z).
Axes of the slice: x: 2, y: 2, z: 4, core: 2. Of those that a mesh axis runs over, the one named last changes fastest.
Arguments:
- tracer: float32 [16, 64, 2880], P(None, 'lat', 'lon'), may hold values from -6 to 6
- zonal_courant: float32 [16, 64, 2880], P(None, 'lat', 'lon'), may hold values from -0.35 to 0.35
- north_courant: float32 [16, 64, 2880], P(None, 'lat', 'lon'), may hold values from -0.35 to 0.35
- cutoff: int32 [16], replicated, may hold values from 1 to 128
Outputs:
- advanced: float32 [16, 64, 2880], P(None, 'lat', 'lon')
All inputs are finite; a program needn't handle non-finite values.
Results may differ from a plain program's by a relative error of at most 0.0001.
Values sent between devices are 32-bit elements; how exact they have to be, the bound alone decides.
A program may use at most 64 MiB of HBM per device.

v0:
```python
import math

import jax
import jax.numpy as jnp
from jax import lax
from jax.sharding import PartitionSpec as P

NLON = 2880
KMAX = 128


DIFFUSION = 0.2


def with_halo(block, sides, width, periodic):
    for axis, dim in sides:
        count = lax.axis_size(axis)
        forward = [(i, i + 1) for i in range(count - 1)]
        if periodic:
            forward.append((count - 1, 0))
        backward = [(target, source) for source, target in forward]
        low = lax.ppermute(
            lax.slice_in_dim(block, block.shape[dim] - width, None, axis=dim), axis, forward
        )
        high = lax.ppermute(lax.slice_in_dim(block, 0, width, axis=dim), axis, backward)
        block = jnp.concatenate([low, block, high], axis=dim)
    return block


def shifted(block, axis, distance):
    devices = range(lax.axis_size(axis))
    route = [((i - distance) % len(devices), i) for i in devices]
    return lax.ppermute(block, axis, route)


def fourier_tables(columns):
    modes = jnp.arange(KMAX, dtype=jnp.int32)
    product = columns[:, None] * modes[None, :] % NLON
    phase_angle = product.astype(jnp.float32) * (2.0 * math.pi / NLON)
    weights = jnp.where(modes == 0, 1.0 / NLON, 2.0 / NLON).astype(jnp.float32)
    cosine = jnp.cos(phase_angle)
    sine = jnp.sin(phase_angle)
    analysis = jnp.concatenate([cosine * weights[None, :], sine * weights[None, :]], axis=1)
    synthesis = jnp.concatenate([cosine, sine], axis=1).T
    return (analysis, synthesis)


def mode_mask(cut_values):
    modes = jnp.arange(KMAX, dtype=jnp.float32)
    doubled = jnp.concatenate([modes, modes])
    return (doubled[None, :] < cut_values[:, None]).astype(jnp.float32)


def shards(tracer, zonal_courant, north_courant, cutoff):
    level_count, row_count, col_count = tracer.shape
    lat_count = lax.axis_size("lat")
    lon_count = lax.axis_size("lon")
    lat_at = lax.axis_index("lat")
    lon_at = lax.axis_index("lon")
    cap_blocks = lat_count // 8
    polar = (lat_at < cap_blocks) | (lat_at >= lat_count - cap_blocks)
    offset = jnp.where(
        lat_at < cap_blocks,
        lat_at * row_count,
        jnp.where(polar, (lat_at - lat_count + 2 * cap_blocks) * row_count, 0),
    )
    row_cut = lax.dynamic_slice_in_dim(cutoff, offset, row_count).astype(jnp.float32)
    flat_count = level_count * row_count
    flat_cut = jnp.broadcast_to(row_cut[None, :], (level_count, row_count)).reshape(flat_count)
    local_columns = lon_at * col_count + jnp.arange(col_count, dtype=jnp.int32)
    analysis, synthesis = fourier_tables(local_columns)
    state = tracer
    for substep in range(2):
        padded = with_halo(state, (("lat", 1),), 1, False)
        edge_rows = jnp.concatenate([state[:, :1], state[:, -1:]], axis=1)
        opposite = shifted(edge_rows, "lon", lon_count // 2)
        south_rim = jnp.where(lat_at == 0, opposite[:, 0], padded[:, 0])
        north_rim = jnp.where(lat_at == lat_count - 1, opposite[:, 1], padded[:, -1])
        padded = jnp.concatenate([south_rim[:, None], padded[:, 1:-1], north_rim[:, None]], axis=1)
        padded = with_halo(padded, (("lon", 2),), 1, True)
        center = padded[:, 1:-1, 1:-1]
        east_cell = padded[:, 1:-1, 2:]
        west_cell = padded[:, 1:-1, :-2]
        north_cell = padded[:, 2:, 1:-1]
        south_cell = padded[:, :-2, 1:-1]
        tendency = (
            -0.5 * zonal_courant * (east_cell - west_cell)
            - 0.5 * north_courant * (north_cell - south_cell)
            + DIFFUSION * (east_cell + west_cell + north_cell + south_cell - 4.0 * center)
        )
        flat_rows = tendency.reshape(flat_count, col_count)
        partial_coeffs = jnp.dot(flat_rows, analysis, precision=lax.Precision.HIGHEST)
        coefficients = lax.psum(partial_coeffs, "lon")
        coefficients = coefficients * mode_mask(flat_cut)
        filtered = jnp.dot(coefficients, synthesis, precision=lax.Precision.HIGHEST)
        filtered = filtered.reshape(level_count, row_count, col_count)
        state = state + jnp.where(polar, filtered, tendency)
    return state


def solution(mesh):
    return jax.shard_map(
        shards,
        mesh=mesh,
        in_specs=(P(None, "lat", "lon"), P(None, "lat", "lon"), P(None, "lat", "lon"), P()),
        out_specs=P(None, "lat", "lon"),
        check_vma=False,
    )
```

profile of v0, /device:TPU:0, one launch (start us, length us, event | category | flops | bytes accessed | tf_op | source)
XLA Modules:
  0.0 136.2 jit_solution(5212779486867433260)
XLA Ops:
  6.5 1.2 fusion.28
  7.7 2.4 %collective-permute-start.1 = (f32[16,1,720]{2,1,0:T(1,128)S(1)}, f32[16,1,720]{2,1,0:T(1,128)S(1)}, u32[]{:S(2)}, u32[]{:S(2)}) collective-permute-start(f32[16,1,720]{2,1,0:T(1,128)S(1)} %get-tuple-element.11), channel_id=1, source_target_pairs={{0,4},{4,8},{8,12},{12,16},{16,20},{20,24},{24,28},{1,5},{5,9},{9,... | collective-permute-start | bytes 138248 | tf_op jit(solution)/shard_map/ppermute | solution.py:22
  10.1 1.3 collective-permute-start.2
  11.5 3.5 %collective-permute-start = (f32[16,2,720]{2,1,0:T(2,128)S(1)}, f32[16,2,720]{2,1,0:T(2,128)S(1)}, u32[]{:S(2)}, u32[]{:S(2)}) collective-permute-start(f32[16,2,720]{2,1,0:T(2,128)S(1)} %pad_maximum_fusion.28), channel_id=1, source_target_pairs={{2,0},{3,1},{0,2},{1,3},{6,4},{7,5},{4,6},{5,7},{10,8},{11,9},{8,1... | collective-permute-start | bytes 276488 | tf_op jit(solution)/shard_map/ppermute | solution.py:33
  15.0 1.6 %broadcast_multiply_fusion.1 = (f32[720,128]{1,0:T(8,128)S(1)}, f32[720,128]{1,0:T(8,128)S(1)}, f32[720,128]{1,0:T(8,128)S(1)}, f32[720,128]{1,0:T(8,128)S(1)}) fusion(f32[128]{0:T(128)S(1)} %compare_select_fusion.4, s32[720]{0:T(1024)S(1)} %iota_add_fusion), kind=kLoop, calls=%fused_computation.40 | loop fusion | flops 1013760 | bytes 1477952 | tf_op jit(solution)/shard_map/mul | solution.py:43
  16.7 0.9 collective-permute-done
  17.9 3.8 %collective-permute-start.4 = (f32[16,10,1]{2,1,0:T(8,128)S(1)}, f32[16,10,1]{2,1,0:T(8,128)S(1)}, u32[]{:S(2)}, u32[]{:S(2)}) collective-permute-start(f32[16,10,1]{2,1,0:T(8,128)S(1)} %get-tuple-element.7), channel_id=1, source_target_pairs={{0,1},{1,2},{2,3},{3,0},{4,5},{5,6},{6,7},{7,4},{8,9},{9,10},{10,1... | collective-permute-start | bytes 1928 | tf_op jit(solution)/shard_map/ppermute | solution.py:22
  21.7 2.9 %collective-permute-start.3 = (f32[16,10,1]{2,1,0:T(8,128)S(1)}, f32[16,10,1]{2,1,0:T(8,128)}, u32[]{:S(2)}, u32[]{:S(2)}) collective-permute-start(f32[16,10,1]{2,1,0:T(8,128)S(1)} %get-tuple-element.8), channel_id=1, source_target_pairs={{1,0},{2,1},{3,2},{0,3},{5,4},{6,5},{7,6},{4,7},{9,8},{10,9},{11,1... | collective-permute-start | bytes 1928 | tf_op jit(solution)/shard_map/ppermute | solution.py:25
  24.6 4.3 %collective-permute-done.4 = f32[16,10,1]{2,1,0:T(8,128)S(1)} collective-permute-done((f32[16,10,1]{2,1,0:T(8,128)S(1)}, f32[16,10,1]{2,1,0:T(8,128)S(1)}, u32[]{:S(2)}, u32[]{:S(2)}) %collective-permute-start.4) | collective-permute-done | bytes 672 | tf_op jit(solution)/shard_map/ppermute | solution.py:22
  28.9 0.7 copy-done.3
  29.6 0.7 collective-permute-done.3
  30.3 1.6 %multiply_add_fusion.1 = f32[16,8,720]{2,1,0:T(8,128)S(1)} fusion(f32[16,8,720]{2,1,0:T(8,128)S(1)} %copy-done, f32[16,1,720]{2,1,0:T(1,128)S(1)} %get-tuple-element.16, f32[16,1,720]{2,1,0:T(1,128)S(1)} %get-tuple-element.15, f32[16,10,1]{2,1,0:T(8,128)} %collective-permute-done.3, f32[16,10,1]{2,1,0:T(8,128)} %copy-done.3, f32[16,8,720]{2,1,0:T(8,128)S(1)} %copy-done.1, ...), kind=kLoop, calls=%fused_computation.30 | loop fusion | flops 2027520 | bytes 1568000 | tf_op jit(solution)/shard_map/add | solution.py:87
  31.8 1.2 fusion.5
  33.9 35.7 %all-reduce.3.cloned.1.call-done = f32[128,256]{1,0:T(8,128)} async-done(((f32[128,256]{1,0:T(8,128)}), f32[128,256]{1,0:T(8,128)}) %all-reduce.3.cloned.1.call-update) | async-done | bytes 131088 | tf_op jit(solution)/shard_map/psum | solution.py:93
  69.5 1.7 %fusion.1 = f32[16,8,720]{2,1,0:T(8,128)S(1)} fusion(f32[16,8,720]{2,1,0:T(8,128)S(1)} %copy-done, f32[16,8,720]{2,1,0:T(8,128)S(1)} %multiply_add_fusion.1, f32[720,128]{1,0:T(8,128)S(1)} %get-tuple-element.19, f32[720,128]{1,0:T(8,128)S(1)} %get-tuple-element.20, pred[]{:T(512)S(6)} %or.3, f32[128,256]{1,0:T(8,128)} %all-reduce.3.cloned.1.call-done, ...), kind=kOutput, calls=%fused_computation.3 | convolution fusion | flops 283549696 | bytes 1975809 | tf_op jit(solution)/shard_map/dot_general | solution.py:95
  71.4 2.1 %collective-permute-start.5 = (f32[16,2,720]{2,1,0:T(2,128)S(1)}, f32[16,2,720]{2,1,0:T(2,128)S(1)}, u32[]{:S(2)}, u32[]{:S(2)}) collective-permute-start(f32[16,2,720]{2,1,0:T(2,128)S(1)} %pad_maximum_fusion.29), channel_id=1, source_target_pairs={{2,0},{3,1},{0,2},{1,3},{6,4},{7,5},{4,6},{5,7},{10,8},{11,9},{8,1... | collective-permute-start | bytes 276488 | tf_op jit(solution)/shard_map/ppermute | solution.py:33
  73.6 1.3 collective-permute-start.6
  74.9 1.3 collective-permute-start.7
  76.2 3.5 %collective-permute-done.7 = f32[16,1,720]{2,1,0:T(1,128)S(1)} collective-permute-done((f32[16,1,720]{2,1,0:T(1,128)S(1)}, f32[16,1,720]{2,1,0:T(1,128)S(1)}, u32[]{:S(2)}, u32[]{:S(2)}) %collective-permute-start.7) | collective-permute-done | bytes 46112 | tf_op jit(solution)/shard_map/ppermute | solution.py:25
  80.6 3.3 %collective-permute-start.8 = (f32[16,10,1]{2,1,0:T(8,128)S(1)}, f32[16,10,1]{2,1,0:T(8,128)S(1)}, u32[]{:S(2)}, u32[]{:S(2)}) collective-permute-start(f32[16,10,1]{2,1,0:T(8,128)S(1)} %get-tuple-element.6), channel_id=1, source_target_pairs={{1,0},{2,1},{3,2},{0,3},{5,4},{6,5},{7,6},{4,7},{9,8},{10,9},{11,1... | collective-permute-start | bytes 1928 | tf_op jit(solution)/shard_map/ppermute | solution.py:25
  83.9 3.0 %collective-permute-done.9 = f32[16,10,1]{2,1,0:T(8,128)S(1)} collective-permute-done((f32[16,10,1]{2,1,0:T(8,128)S(1)}, f32[16,10,1]{2,1,0:T(8,128)S(1)}, u32[]{:S(2)}, u32[]{:S(2)}) %collective-permute-start.9) | collective-permute-done | bytes 672 | tf_op jit(solution)/shard_map/ppermute | solution.py:22
  87.7 1.2 fusion.4
  88.9 38.0 %all-reduce.5.cloned.1.call-done = f32[128,256]{1,0:T(8,128)} async-done(((f32[128,256]{1,0:T(8,128)}), f32[128,256]{1,0:T(8,128)}) %all-reduce.5.cloned.1.call-update) | async-done | bytes 131088 | tf_op jit(solution)/shard_map/psum | solution.py:93
  126.9 2.5 %fusion.3 = f32[16,8,720]{2,1,0:T(8,128)} fusion(f32[16,8,720]{2,1,0:T(8,128)S(1)} %fusion.1, f32[16,8,720]{2,1,0:T(8,128)S(1)} %multiply_add_fusion, f32[720,128]{1,0:T(8,128)S(1)} %get-tuple-element.19, f32[720,128]{1,0:T(8,128)S(1)} %get-tuple-element.20, pred[]{:T(512)S(6)} %or.3, f32[128,256]{1,0:T(8,128)} %all-reduce.5.cloned.1.call-done, ...), kind=kOutput, calls=%fused_computation.5 | convolution fusion | flops 283549696 | bytes 1975809 | tf_op jit(solution)/shard_map/dot_general | solution.py:95
  (34 shorter events, 3.0 us)
Async XLA Ops:
  6.5 63.0 %all-reduce.3.cloned.1.call-start = ((), (), s32[]{:S(2)}) async-start(), calls=%async_computation | async-start | bytes 262144 | tf_op jit(solution)/shard_map/psum | solution.py:93
  7.7 8.9 %collective-permute-start.1 = (f32[16,1,720]{2,1,0:T(1,128)S(1)}, f32[16,1,720]{2,1,0:T(1,128)S(1)}, u32[]{:S(2)}, u32[]{:S(2)}) collective-permute-start(f32[16,1,720]{2,1,0:T(1,128)S(1)} %get-tuple-element.11), channel_id=1, source_target_pairs={{0,4},{4,8},{8,12},{12,16},{16,20},{20,24},{24,28},{1,5},{5,9},{9,... | collective-permute-start | bytes 138248 | tf_op jit(solution)/shard_map/ppermute | solution.py:22
  10.1 6.5 %collective-permute-start.2 = (f32[16,1,720]{2,1,0:T(1,128)S(1)}, f32[16,1,720]{2,1,0:T(1,128)S(1)}, u32[]{:S(2)}, u32[]{:S(2)}) collective-permute-start(f32[16,1,720]{2,1,0:T(1,128)S(1)} %get-tuple-element.12), channel_id=1, source_target_pairs={{4,0},{8,4},{12,8},{16,12},{20,16},{24,20},{28,24},{5,1},{9,5},{13... | collective-permute-start | bytes 138248 | tf_op jit(solution)/shard_map/ppermute | solution.py:25
  11.5 6.1 %collective-permute-start = (f32[16,2,720]{2,1,0:T(2,128)S(1)}, f32[16,2,720]{2,1,0:T(2,128)S(1)}, u32[]{:S(2)}, u32[]{:S(2)}) collective-permute-start(f32[16,2,720]{2,1,0:T(2,128)S(1)} %pad_maximum_fusion.28), channel_id=1, source_target_pairs={{2,0},{3,1},{0,2},{1,3},{6,4},{7,5},{4,6},{5,7},{10,8},{11,9},{8,1... | collective-permute-start | bytes 276488 | tf_op jit(solution)/shard_map/ppermute | solution.py:33
  15.0 2.7 %copy-start = (f32[16,8,720]{2,1,0:T(8,128)S(1)}, f32[16,8,720]{2,1,0:T(8,128)}, u32[]{:S(2)}) copy-start(f32[16,8,720]{2,1,0:T(8,128)} %param.4) | copy-start | bytes 1105924
  17.6 12.7 %copy-start.2 = (f32[16,8,720]{2,1,0:T(8,128)S(1)}, f32[16,8,720]{2,1,0:T(8,128)}, u32[]{:S(2)}) copy-start(f32[16,8,720]{2,1,0:T(8,128)} %param.5) | copy-start | bytes 1105924
  17.7 12.5 %copy-start.1 = (f32[16,8,720]{2,1,0:T(8,128)S(1)}, f32[16,8,720]{2,1,0:T(8,128)}, u32[]{:S(2)}) copy-start(f32[16,8,720]{2,1,0:T(8,128)} %param.6) | copy-start | bytes 1105924
  17.9 11.0 %collective-permute-start.4 = (f32[16,10,1]{2,1,0:T(8,128)S(1)}, f32[16,10,1]{2,1,0:T(8,128)S(1)}, u32[]{:S(2)}, u32[]{:S(2)}) collective-permute-start(f32[16,10,1]{2,1,0:T(8,128)S(1)} %get-tuple-element.7), channel_id=1, source_target_pairs={{0,1},{1,2},{2,3},{3,0},{4,5},{5,6},{6,7},{7,4},{8,9},{9,10},{10,1... | collective-permute-start | bytes 1928 | tf_op jit(solution)/shard_map/ppermute | solution.py:22
  21.7 8.5 %collective-permute-start.3 = (f32[16,10,1]{2,1,0:T(8,128)S(1)}, f32[16,10,1]{2,1,0:T(8,128)}, u32[]{:S(2)}, u32[]{:S(2)}) collective-permute-start(f32[16,10,1]{2,1,0:T(8,128)S(1)} %get-tuple-element.8), channel_id=1, source_target_pairs={{1,0},{2,1},{3,2},{0,3},{5,4},{6,5},{7,6},{4,7},{9,8},{10,9},{11,1... | collective-permute-start | bytes 1928 | tf_op jit(solution)/shard_map/ppermute | solution.py:25
  28.9 0.7 copy-start.3
  33.0 0.7 copy-start.4
  33.0 93.9 %all-reduce.5.cloned.1.call-start = ((), (), s32[]{:S(2)}) async-start(), calls=%async_computation.1 | async-start | bytes 262144 | tf_op jit(solution)/shard_map/psum | solution.py:93
  71.4 8.3 %collective-permute-start.5 = (f32[16,2,720]{2,1,0:T(2,128)S(1)}, f32[16,2,720]{2,1,0:T(2,128)S(1)}, u32[]{:S(2)}, u32[]{:S(2)}) collective-permute-start(f32[16,2,720]{2,1,0:T(2,128)S(1)} %pad_maximum_fusion.29), channel_id=1, source_target_pairs={{2,0},{3,1},{0,2},{1,3},{6,4},{7,5},{4,6},{5,7},{10,8},{11,9},{8,1... | collective-permute-start | bytes 276488 | tf_op jit(solution)/shard_map/ppermute | solution.py:33
  73.6 2.6 %collective-permute-start.6 = (f32[16,1,720]{2,1,0:T(1,128)S(1)}, f32[16,1,720]{2,1,0:T(1,128)S(1)}, u32[]{:S(2)}, u32[]{:S(2)}) collective-permute-start(f32[16,1,720]{2,1,0:T(1,128)S(1)} %get-tuple-element.9), channel_id=1, source_target_pairs={{0,4},{4,8},{8,12},{12,16},{16,20},{20,24},{24,28},{1,5},{5,9},{9,... | collective-permute-start | bytes 138248 | tf_op jit(solution)/shard_map/ppermute | solution.py:22
  74.9 4.9 %collective-permute-start.7 = (f32[16,1,720]{2,1,0:T(1,128)S(1)}, f32[16,1,720]{2,1,0:T(1,128)S(1)}, u32[]{:S(2)}, u32[]{:S(2)}) collective-permute-start(f32[16,1,720]{2,1,0:T(1,128)S(1)} %get-tuple-element.10), channel_id=1, source_target_pairs={{4,0},{8,4},{12,8},{16,12},{20,16},{24,20},{28,24},{5,1},{9,5},{13... | collective-permute-start | bytes 138248 | tf_op jit(solution)/shard_map/ppermute | solution.py:25
  80.0 6.9 %collective-permute-start.9 = (f32[16,10,1]{2,1,0:T(8,128)S(1)}, f32[16,10,1]{2,1,0:T(8,128)S(1)}, u32[]{:S(2)}, u32[]{:S(2)}) collective-permute-start(f32[16,10,1]{2,1,0:T(8,128)S(1)} %get-tuple-element.5), channel_id=1, source_target_pairs={{0,1},{1,2},{2,3},{3,0},{4,5},{5,6},{6,7},{7,4},{8,9},{9,10},{10,1... | collective-permute-start | bytes 1928 | tf_op jit(solution)/shard_map/ppermute | solution.py:22
  80.6 6.4 %collective-permute-start.8 = (f32[16,10,1]{2,1,0:T(8,128)S(1)}, f32[16,10,1]{2,1,0:T(8,128)S(1)}, u32[]{:S(2)}, u32[]{:S(2)}) collective-permute-start(f32[16,10,1]{2,1,0:T(8,128)S(1)} %get-tuple-element.6), channel_id=1, source_target_pairs={{1,0},{2,1},{3,2},{0,3},{5,4},{6,5},{7,6},{4,7},{9,8},{10,9},{11,1... | collective-permute-start | bytes 1928 | tf_op jit(solution)/shard_map/ppermute | solution.py:25
Sparse Core Ops, SparseCore 0:
  33.1 36.3 all-reduce.2
  89.0 37.8 all-reduce.4
where the time goes:
time: 136 us
  waiting for transfers between devices  86.4 us (64%)
  starting transfers between devices  22.5 us (17%)
  between operations  13.6 us (10%)
  matrix products  6.6 us (5%)
  other arithmetic  4.59 us (3%)
  local copies, waits for them, and re-layouts  2.6 us (2%)
    psum x2, waiting for transfers between devices, shards(): coefficients = lax.psum(partial_coeffs, 'lon')  73.7 us
    ppermute x4, starting transfers between devices, with_halo(): lax.ppermute(lax.slice_in_dim(block, 0, width, axis=dim), axis, backward)  8.73 us
    ppermute x4, starting transfers between devices, with_halo(): lax.ppermute(lax.slice_in_dim(block, block.shape[dim] - width, None, axis...  8.12 us
    ppermute x4, waiting for transfers between devices, with_halo(): lax.ppermute(lax.slice_in_dim(block, block.shape[dim] - width, None, axis...  7.37 us
    ppermute x2, starting transfers between devices, shifted(): return lax.ppermute(block, axis, route)  5.61 us
    ppermute x4, waiting for transfers between devices, with_halo(): lax.ppermute(lax.slice_in_dim(block, 0, width, axis=dim), axis, backward)  4.34 us
    dot_general x2, matrix products, shards(): filtered = jnp.dot(coefficients, synthesis, precision=lax.Precision.HIGHEST)  4.25 us
  transfers between devices with their start and end apart: 12, of which 8 were waited for; matrix products, arithmetic and copies ran while one was open for 1% of the time, Pallas kernels for 0%

commit v1 on v0

v1 whole, which is shorter than its diff:
```python
import functools
import math

import jax
import jax.numpy as jnp
import numpy as np
from jax import lax
from jax.experimental import pallas as pl
from jax.experimental.pallas import tpu as pltpu
from jax.sharding import PartitionSpec as P

KMAX = 128
DIFFUSION = 0.2
LANES = 128
MESH = pl.DeviceIdType.MESH
F32 = jnp.float32
BF16 = jnp.bfloat16


def split_table(table):
    high = table.astype(np.float32).astype(BF16)
    low = (table - high.astype(np.float64)).astype(np.float32).astype(BF16)
    return np.stack([high, low])


def tables(cols, width, lon_count):
    lane = np.arange(width)
    lane = np.where(lane == width - 1, -1, lane)
    modes = np.arange(KMAX)
    total = cols * lon_count
    angle = (lane[:, None] * modes[None, :] % total) * (2.0 * math.pi / total)
    both = np.concatenate([np.cos(angle), np.sin(angle)], axis=1)
    block = np.arange(lon_count) * cols
    turn = (block[:, None] * modes[None, :] % total) * (2.0 * math.pi / total)
    phase = np.zeros((lon_count, 8, KMAX), np.float32)
    phase[:, 0] = np.cos(turn)
    phase[:, 1] = np.sin(turn)
    return split_table(both), split_table(both.T.copy()), phase


def split(value):
    high = value.astype(BF16)
    low = (value - high.astype(F32)).astype(BF16)
    return high, low


def dot3(value, table):
    high, low = split(value)
    t_high = table[0]
    t_low = table[1]
    dot = functools.partial(jnp.dot, preferred_element_type=F32)
    return dot(high, t_high) + (dot(low, t_high) + dot(high, t_low))


def kernel(
    lat_count, lon_count, cap_blocks,
    cut_ref, tracer, zonal, north, ana_hbm, syn_hbm, phase_hbm, out_hbm,
    q_in, zc, nc, ana, syn, phase, out, q, tend,
    row_out, row_in, col_out, col_in, pole_in,
    part, part_in, coef,
    load_sem, row_send, row_recv, col_send, col_recv, pole_send, pole_recv,
    rs_send, rs_recv, ag_send, ag_recv,
):
    levels, rows, cols = q_in.shape
    width = q.shape[2]
    total = cols * lon_count
    per = levels // lon_count
    lat = lax.axis_index("lat")
    lon = lax.axis_index("lon")
    polar = jnp.logical_or(lat < cap_blocks, lat >= lat_count - cap_blocks)
    first = lat == 0
    last = lat == lat_count - 1
    east = lax.rem(lon + 1, lon_count)
    west = lax.rem(lon + lon_count - 1, lon_count)
    across = lax.rem(lon + lon_count // 2, lon_count)

    loads = [
        pltpu.make_async_copy(tracer, q_in, load_sem.at[0]),
        pltpu.make_async_copy(zonal, zc, load_sem.at[1]),
        pltpu.make_async_copy(north, nc, load_sem.at[2]),
        pltpu.make_async_copy(ana_hbm, ana, load_sem.at[3]),
        pltpu.make_async_copy(syn_hbm, syn, load_sem.at[4]),
        pltpu.make_async_copy(phase_hbm.at[lon], phase, load_sem.at[5]),
    ]
    for load in loads:
        load.start()

    barrier = pltpu.get_barrier_semaphore()

    def greet(there):
        pl.semaphore_signal(barrier, inc=1, device_id=there, device_id_type=MESH)

    @pl.when(jnp.logical_not(first))
    def _():
        greet({"lat": lat - 1, "lon": lon})

    @pl.when(jnp.logical_not(last))
    def _():
        greet({"lat": lat + 1, "lon": lon})

    @pl.when(polar)
    def _():
        for step in range(1, lon_count):
            greet({"lat": lat, "lon": lax.rem(lon + step, lon_count)})

    @pl.when(jnp.logical_not(polar))
    def _():
        greet({"lat": lat, "lon": east})
        greet({"lat": lat, "lon": west})

    lane = lax.broadcasted_iota(jnp.int32, (rows, LANES), 1)
    row_at = lax.broadcasted_iota(jnp.int32, (rows, width), 0)

    def row_copy(turn, side):
        there = lat + 1 if side == 0 else lat - 1
        return pltpu.make_async_remote_copy(
            row_out.at[turn, side], row_in.at[turn, side],
            row_send.at[turn, side], row_recv.at[turn, side],
            device_id={"lat": there, "lon": lon}, device_id_type=MESH)

    def col_copy(turn, side):
        return pltpu.make_async_remote_copy(
            col_out.at[turn, side], col_in.at[turn, side],
            col_send.at[turn, side], col_recv.at[turn, side],
            device_id={"lat": lat, "lon": east if side == 0 else west}, device_id_type=MESH)

    def pole_copy(side):
        return pltpu.make_async_remote_copy(
            row_out.at[0, side], pole_in, pole_send, pole_recv,
            device_id={"lat": lat, "lon": across}, device_id_type=MESH)

    def rs_copy(turn, step):
        there = lax.rem(lon + step, lon_count)
        return pltpu.make_async_remote_copy(
            part.at[turn, pl.ds(there * per, per)], part_in.at[turn, step - 1],
            rs_send.at[turn, step - 1], rs_recv.at[turn, step - 1],
            device_id={"lat": lat, "lon": there}, device_id_type=MESH)

    def ag_copy(turn, step):
        there = lax.rem(lon + step, lon_count)
        mine = coef.at[turn, pl.ds(lon * per, per)]
        return pltpu.make_async_remote_copy(
            mine, mine, ag_send.at[turn, step - 1], ag_recv.at[turn, step - 1],
            device_id={"lat": lat, "lon": there}, device_id_type=MESH)

    def ag_arrival(turn, step):
        origin = lax.rem(lon + lon_count - step, lon_count)
        theirs = coef.at[turn, pl.ds(origin * per, per)]
        return pltpu.make_async_remote_copy(
            theirs, theirs, ag_send.at[turn, step - 1], ag_recv.at[turn, step - 1],
            device_id={"lat": lat, "lon": origin}, device_id_type=MESH)

    def pack_rows(turn):
        row_out[turn, 0] = q[:, rows - 1, :]
        row_out[turn, 1] = q[:, 0, :]

    def pack_cols(turn):
        end_tile = (cols - 1) // LANES * LANES
        high = jnp.zeros((rows, LANES), F32)
        low = jnp.zeros((rows, LANES), F32)
        for level in range(levels):
            tile = q[level, :, end_tile:end_tile + LANES]
            high = jnp.where(lane == level, pltpu.roll(tile, (level - (cols - 1) % LANES) % LANES, 1), high)
            tile = q[level, :, 0:LANES]
            low = jnp.where(lane == level, pltpu.roll(tile, level, 1) if level else tile, low)
        col_out[turn, 0] = high
        col_out[turn, 1] = low

    def place_cols(turn):
        from_west = col_in[turn, 0]
        from_east = col_in[turn, 1]
        east_tile = cols // LANES * LANES
        west_tile = width - LANES
        for level in range(levels):
            tile = q[level, :, east_tile:east_tile + LANES]
            moved = pltpu.roll(from_east, (cols % LANES - level) % LANES, 1)
            q[level, :, east_tile:east_tile + LANES] = jnp.where(lane == cols % LANES, moved, tile)
            tile = q[level, :, west_tile:west_tile + LANES]
            moved = pltpu.roll(from_west, (LANES - 1 - level) % LANES, 1)
            q[level, :, west_tile:west_tile + LANES] = jnp.where(lane == LANES - 1, moved, tile)

    def stencil(turn, level):
        here = q[level]
        to_east = pltpu.roll(here, width - 1, 1)
        to_west = pltpu.roll(here, 1, 1)
        top = row_in[turn, 1, pl.ds(level, 1), :]
        bottom = row_in[turn, 0, pl.ds(level, 1), :]
        to_north = jnp.where(row_at == rows - 1, top, pltpu.roll(here, rows - 1, 0))
        to_south = jnp.where(row_at == 0, bottom, pltpu.roll(here, 1, 0))
        here, to_east, to_west, to_north, to_south = (
            value[:, :cols] for value in (here, to_east, to_west, to_north, to_south))
        return (-0.5 * zc[level] * (to_east - to_west)
                - 0.5 * nc[level] * (to_north - to_south)
                + DIFFUSION * (to_east + to_west + to_north + to_south - 4.0 * here))

    q[:, :, (width - LANES):] = jnp.zeros((levels, rows, LANES), F32)
    loads[0].wait()
    for level in range(levels):
        q[level, :, :cols] = q_in[level]
    pack_rows(0)
    pack_cols(0)

    ends = first.astype(jnp.int32) + last.astype(jnp.int32)
    sides = jnp.where(polar, lon_count - 1, 2)
    pl.semaphore_wait(barrier, 2 - ends + sides)

    @pl.when(jnp.logical_not(last))
    def _():
        row_copy(0, 0).start()

    @pl.when(jnp.logical_not(first))
    def _():
        row_copy(0, 1).start()

    @pl.when(last)
    def _():
        pole_copy(0).start()

    @pl.when(first)
    def _():
        pole_copy(1).start()

    col_copy(0, 0).start()
    col_copy(0, 1).start()

    offset = jnp.where(
        lat < cap_blocks, lat * rows,
        jnp.where(polar, (lat - lat_count + 2 * cap_blocks) * rows, 0))
    tend[...] = jnp.zeros_like(tend)
    for load in loads[1:]:
        load.wait()

    @pl.when(jnp.logical_not(last))
    def _():
        row_copy(0, 1).wait_recv()
        row_copy(0, 0).wait_send()

    @pl.when(jnp.logical_not(first))
    def _():
        row_copy(0, 0).wait_recv()
        row_copy(0, 1).wait_send()

    @pl.when(last)
    def _():
        pole_copy(0).wait()
        row_in[0, 1] = pole_in[...]

    @pl.when(first)
    def _():
        pole_copy(1).wait()
        row_in[0, 0] = pole_in[...]

    col_copy(0, 0).wait()
    col_copy(0, 1).wait()
    place_cols(0)

    @pl.when(jnp.logical_not(polar))
    def _():
        for level in range(levels):
            tend[level, :, :cols] = stencil(0, level)
        for level in range(levels):
            q[level, :, :cols] = q[level, :, :cols] + tend[level, :, :cols]
        pack_rows(1)
        row_copy(1, 0).start()
        row_copy(1, 1).start()
        pack_cols(1)
        col_copy(1, 0).start()
        col_copy(1, 1).start()
        row_copy(1, 0).wait()
        row_copy(1, 1).wait()
        col_copy(1, 0).wait()
        col_copy(1, 1).wait()
        place_cols(1)
        for level in range(levels):
            out[level] = q[level, :, :cols] + stencil(1, level)

    @pl.when(polar)
    def _():
        mode = lax.broadcasted_iota(jnp.int32, (rows, KMAX), 1)
        which = lax.broadcasted_iota(jnp.int32, (rows, KMAX), 0)
        weight = jnp.where(mode == 0, 1.0 / total, 2.0 / total).astype(F32)
        cut = jnp.zeros((rows, KMAX), jnp.int32)
        for row in range(rows):
            cut = jnp.where(which == row, cut_ref[offset + row], cut)
        keep = jnp.where(mode < cut, weight, 0.0)[None]
        cosine = phase[0:1, :]
        sine = phase[1:2, :]
        parity = 1.0 - 2.0 * (lax.broadcasted_iota(jnp.int32, (1, 2 * KMAX), 1) % 2).astype(F32)

        def filtered_coefficients(turn):
            partial = dot3(tend[...].reshape(levels * rows, width), ana)
            real = partial[:, :KMAX]
            imag = partial[:, KMAX:]
            part[turn, :, :, :KMAX] = (real * cosine - imag * sine).reshape(levels, rows, KMAX)
            part[turn, :, :, KMAX:] = (real * sine + imag * cosine).reshape(levels, rows, KMAX)
            for step in range(1, lon_count):
                rs_copy(turn, step).start()
            summed = part[turn, pl.ds(lon * per, per)]
            for step in range(1, lon_count):
                rs_copy(turn, step).wait_recv()
                summed = summed + part_in[turn, step - 1]
            coef[turn, pl.ds(lon * per, per), :, :KMAX] = summed[:, :, :KMAX] * keep
            coef[turn, pl.ds(lon * per, per), :, KMAX:] = summed[:, :, KMAX:] * keep
            for step in range(1, lon_count):
                ag_copy(turn, step).start()
            for step in range(1, lon_count):
                rs_copy(turn, step).wait_send()
            for step in range(1, lon_count):
                ag_arrival(turn, step).wait_recv()
            for step in range(1, lon_count):
                ag_copy(turn, step).wait_send()
            sums = coef[turn].reshape(levels * rows, 2 * KMAX)
            real = sums[:, :KMAX]
            imag = sums[:, KMAX:]
            return jnp.concatenate(
                [real * cosine + imag * sine, imag * cosine - real * sine], axis=1)

        for level in range(levels):
            tend[level, :, :cols] = stencil(0, level)
        local = filtered_coefficients(0)
        filtered = dot3(local, syn)
        q[...] = q[...] + filtered.reshape(levels, rows, width)
        pack_rows(1)

        @pl.when(jnp.logical_not(last))
        def _():
            row_copy(1, 0).start()

        @pl.when(jnp.logical_not(first))
        def _():
            row_copy(1, 1).start()

        by_level = local.reshape(levels, rows, 2 * KMAX)
        pole_row = jnp.where(first, by_level[:, 0, :], by_level[:, rows - 1, :]) * parity
        pole_sum = pole_in[...] + dot3(pole_row, syn)

        @pl.when(last)
        def _():
            row_in[1, 1] = pole_sum

        @pl.when(first)
        def _():
            row_in[1, 0] = pole_sum

        @pl.when(jnp.logical_not(last))
        def _():
            row_copy(1, 1).wait_recv()
            row_copy(1, 0).wait_send()

        @pl.when(jnp.logical_not(first))
        def _():
            row_copy(1, 0).wait_recv()
            row_copy(1, 1).wait_send()

        for level in range(levels):
            tend[level, :, :cols] = stencil(1, level)
        filtered = dot3(filtered_coefficients(1), syn)
        filtered = filtered.reshape(levels, rows, width)
        for level in range(levels):
            out[level] = q[level, :, :cols] + filtered[level, :, :cols]

    store = pltpu.make_async_copy(out, out_hbm, load_sem.at[0])
    store.start()
    store.wait()


def shards(tracer, zonal_courant, north_courant, cutoff):
    levels, rows, cols = tracer.shape
    lat_count = lax.axis_size("lat")
    lon_count = lax.axis_size("lon")
    cap_blocks = lat_count // 8
    width = -(-(cols + 2) // LANES) * LANES
    per = levels // lon_count
    analysis, synthesis, phase = tables(cols, width, lon_count)
    peers = lon_count - 1
    dma = pltpu.SemaphoreType.DMA
    anywhere = pl.BlockSpec(memory_space=pl.ANY)
    return pl.pallas_call(
        functools.partial(kernel, lat_count, lon_count, cap_blocks),
        out_shape=jax.ShapeDtypeStruct(tracer.shape, F32),
        in_specs=[pl.BlockSpec(memory_space=pltpu.SMEM)] + [anywhere] * 6,
        out_specs=anywhere,
        scratch_shapes=[
            pltpu.VMEM((levels, rows, cols), F32),
            pltpu.VMEM((levels, rows, cols), F32),
            pltpu.VMEM((levels, rows, cols), F32),
            pltpu.VMEM(analysis.shape, BF16),
            pltpu.VMEM(synthesis.shape, BF16),
            pltpu.VMEM(phase.shape[1:], F32),
            pltpu.VMEM((levels, rows, cols), F32),
            pltpu.VMEM((levels, rows, width), F32),
            pltpu.VMEM((levels, rows, width), F32),
            pltpu.VMEM((2, 2, levels, width), F32),
            pltpu.VMEM((2, 2, levels, width), F32),
            pltpu.VMEM((2, 2, rows, LANES), F32),
            pltpu.VMEM((2, 2, rows, LANES), F32),
            pltpu.VMEM((levels, width), F32),
            pltpu.VMEM((2, levels, rows, 2 * KMAX), F32),
            pltpu.VMEM((2, peers, per, rows, 2 * KMAX), F32),
            pltpu.VMEM((2, levels, rows, 2 * KMAX), F32),
            dma((6,)),
            dma((2, 2)), dma((2, 2)), dma((2, 2)), dma((2, 2)),
            dma(()), dma(()),
            dma((2, peers)), dma((2, peers)), dma((2, peers)), dma((2, peers)),
        ],
        compiler_params=pltpu.CompilerParams(collective_id=0, has_side_effects=True),
    )(cutoff, tracer, zonal_courant, north_courant,
      jnp.asarray(analysis), jnp.asarray(synthesis), jnp.asarray(phase))


def solution(mesh):
    return jax.shard_map(
        shards,
        mesh=mesh,
        in_specs=(P(None, "lat", "lon"), P(None, "lat", "lon"), P(None, "lat", "lon"), P()),
        out_specs=P(None, "lat", "lon"),
        check_vma=False,
    )
```

time: 136 us -> 32.2 us (0.24)
  waiting for transfers between devices: 86.4 us -> 0 us
  Pallas kernels: 0 us -> 30.3 us
  starting transfers between devices: 22.5 us -> 0 us
  between operations: 13.6 us -> 0.01 us
  matrix products: 6.6 us -> 0 us
  other arithmetic: 4.59 us -> 0 us
    psum x2 -> x0, waiting for transfers between devices: 73.7 us -> none  [shards(): coefficients = lax.psum(partial_coeffs, 'lon')]
    pallas_call x0 -> x1, Pallas kernels: none -> 30.3 us  [shards(): pl.pallas_call(functools.partial(kernel, lat_count, lon_count, cap_blocks...]
    ppermute x10 -> x0, starting transfers between devices: 22.5 us -> none  [the longest x4 8.73 us: with_halo(): lax.ppermute(lax.slice_in_dim(block, 0, width, axis=dim), axis, backward)]
    ppermute x10 -> x0, waiting for transfers between devices: 12.7 us -> none  [the longest x4 7.37 us: with_halo(): lax.ppermute(lax.slice_in_dim(block, block.shape[dim] - width, None, axis...]
    dot_general x4 -> x0, matrix products: 6.6 us -> none  [the longest x2 4.25 us: shards(): filtered = jnp.dot(coefficients, synthesis, precision=lax.Precision.HIGHEST)]
    add x3 -> x0, other arithmetic: 2.19 us -> none  [the longest x2 2.18 us: shards(): -0.5 * zonal_courant * (east_cell - west_cell)]
    mul x1 -> x0, other arithmetic: 1.62 us -> none  [fourier_tables(): cosine * weights[None, :]]
  transfers between devices with their start and end apart: 12 -> 0, of which waited for: 8 -> 0; matrix products, arithmetic and copies ran while one was open for 1% -> 0% of each run, Pallas kernels for 0% -> 0%
where the time goes in v1:
time: 32.2 us; the launch traced here: 32 us
  Pallas kernels  30.3 us (94%)
  local copies, waits for them, and re-layouts  1.77 us (5%)
    pallas_call x1, Pallas kernels, shards(): pl.pallas_call(functools.partial(kernel, lat_count, lon_count, cap_blocks...  30.3 us
    unnamed x1, local copies, waits for them, and re-layouts  1.77 us

profile of v1, /device:TPU:0, one launch (start us, length us, event | category | flops | bytes accessed | tf_op | source)
XLA Modules:
  0.0 32.0 jit_solution(8842773960511636391)
XLA Ops:
  0.0 30.3 %shard_map.73 = f32[16,8,720]{2,1,0:T(8,128)} custom-call(s32[16]{0:T(128)} %cut_ref.1, f32[16,8,720]{2,1,0:T(8,128)} %tracer.1, f32[16,8,720]{2,1,0:T(8,128)} %zonal.1, f32[16,8,720]{2,1,0:T(8,128)} %north.1, bf16[2,768,256]{2,1,0:T(8,128)(2,1)} %constant.6.clone.ana_hbm, bf16[2,256,768]{2,1,0:T(8,128)(2,1)} %constant.7.clone.syn_hbm, ...), custom_call_target="tpu_custom_call" | custom-call | tf_op jit(solution)/shard_map/pallas_call | solution.py:378
  30.3 1.8 %copy.9 = f32[16,8,720]{2,1,0:T(8,128)} copy(f32[16,8,720]{2,1,0:T(8,128)} %shard_map.73) | data formatting | bytes 737280

commit v2 on v1

--- a/solution.py
+++ b/solution.py
@@ -11,6 +11,7 @@
 
 KMAX = 128
 DIFFUSION = 0.2
+PIECES = 1
 LANES = 128
 MESH = pl.DeviceIdType.MESH
 F32 = jnp.float32
@@ -54,17 +55,17 @@
 
 def kernel(
     lat_count, lon_count, cap_blocks,
-    cut_ref, tracer, zonal, north, ana_hbm, syn_hbm, phase_hbm, out_hbm,
-    q_in, zc, nc, ana, syn, phase, out, q, tend,
+    cut_ref, tracer, zonal, north, ana_hbm, syn_hbm, phase_hbm, out,
+    q_in, zc, nc, ana, syn, phase, q, tend,
     row_out, row_in, col_out, col_in, pole_in,
-    part, part_in, coef,
+    part, part_in,
     load_sem, row_send, row_recv, col_send, col_recv, pole_send, pole_recv,
-    rs_send, rs_recv, ag_send, ag_recv,
+    sum_send, sum_recv,
 ):
     levels, rows, cols = q_in.shape
     width = q.shape[2]
     total = cols * lon_count
-    per = levels // lon_count
+    per = levels // PIECES
     lat = lax.axis_index("lat")
     lon = lax.axis_index("lon")
     polar = jnp.logical_or(lat < cap_blocks, lat >= lat_count - cap_blocks)
@@ -82,8 +83,7 @@
         pltpu.make_async_copy(syn_hbm, syn, load_sem.at[4]),
         pltpu.make_async_copy(phase_hbm.at[lon], phase, load_sem.at[5]),
     ]
-    for load in loads:
-        load.start()
+    loads[0].start()
 
     barrier = pltpu.get_barrier_semaphore()
 
@@ -129,26 +129,27 @@
             row_out.at[0, side], pole_in, pole_send, pole_recv,
             device_id={"lat": lat, "lon": across}, device_id_type=MESH)
 
-    def rs_copy(turn, step):
-        there = lax.rem(lon + step, lon_count)
+    def sum_copy(turn, piece, target):
         return pltpu.make_async_remote_copy(
-            part.at[turn, pl.ds(there * per, per)], part_in.at[turn, step - 1],
-            rs_send.at[turn, step - 1], rs_recv.at[turn, step - 1],
-            device_id={"lat": lat, "lon": there}, device_id_type=MESH)
-
-    def ag_copy(turn, step):
-        there = lax.rem(lon + step, lon_count)
-        mine = coef.at[turn, pl.ds(lon * per, per)]
+            part.at[turn, pl.ds(piece * per, per)], part_in.at[turn, lon, pl.ds(piece * per, per)],
+            sum_send.at[turn, piece, target], sum_recv.at[turn, piece, lon],
+            device_id={"lat": lat, "lon": target}, device_id_type=MESH)
+
+    def sum_arrival(turn, piece, source):
+        theirs = part_in.at[turn, source, pl.ds(piece * per, per)]
         return pltpu.make_async_remote_copy(
-            mine, mine, ag_send.at[turn, step - 1], ag_recv.at[turn, step - 1],
-            device_id={"lat": lat, "lon": there}, device_id_type=MESH)
-
-    def ag_arrival(turn, step):
-        origin = lax.rem(lon + lon_count - step, lon_count)
-        theirs = coef.at[turn, pl.ds(origin * per, per)]
-        return pltpu.make_async_remote_copy(
-            theirs, theirs, ag_send.at[turn, step - 1], ag_recv.at[turn, step - 1],
-            device_id={"lat": lat, "lon": origin}, device_id_type=MESH)
+            theirs, theirs, sum_send.at[turn, piece, source], sum_recv.at[turn, piece, source],
+            device_id={"lat": lat, "lon": source}, device_id_type=MESH)
+
+    def send_sums(turn, piece):
+        for distance in range(lon_count - 1, 0, -1):
+            @pl.when(lon + distance < lon_count)
+            def _():
+                sum_copy(turn, piece, lon + distance).start()
+
+            @pl.when(lon - distance >= 0)
+            def _():
+                sum_copy(turn, piece, lon - distance).start()
 
     def pack_rows(turn):
         row_out[turn, 0] = q[:, rows - 1, :]
@@ -195,6 +196,8 @@
 
     q[:, :, (width - LANES):] = jnp.zeros((levels, rows, LANES), F32)
     loads[0].wait()
+    for load in loads[1:]:
+        load.start()
     for level in range(levels):
         q[level, :, :cols] = q_in[level]
     pack_rows(0)
@@ -287,39 +290,43 @@
         sine = phase[1:2, :]
         parity = 1.0 - 2.0 * (lax.broadcasted_iota(jnp.int32, (1, 2 * KMAX), 1) % 2).astype(F32)
 
-        def filtered_coefficients(turn):
-            partial = dot3(tend[...].reshape(levels * rows, width), ana)
+        def analyse(turn, piece):
+            here = slice(piece * per, (piece + 1) * per)
+            for level in range(piece * per, (piece + 1) * per):
+                tend[level, :, :cols] = stencil(turn, level)
+            partial = dot3(tend[here].reshape(per * rows, width), ana)
             real = partial[:, :KMAX]
             imag = partial[:, KMAX:]
-            part[turn, :, :, :KMAX] = (real * cosine - imag * sine).reshape(levels, rows, KMAX)
-            part[turn, :, :, KMAX:] = (real * sine + imag * cosine).reshape(levels, rows, KMAX)
+            part[turn, here, :, :KMAX] = (real * cosine - imag * sine).reshape(per, rows, KMAX)
+            part[turn, here, :, KMAX:] = (real * sine + imag * cosine).reshape(per, rows, KMAX)
+            send_sums(turn, piece)
+
+        def collect(turn, piece):
+            here = slice(piece * per, (piece + 1) * per)
             for step in range(1, lon_count):
-                rs_copy(turn, step).start()
-            summed = part[turn, pl.ds(lon * per, per)]
+                sum_arrival(turn, piece, lax.rem(lon + step, lon_count)).wait_recv()
+            summed = part[turn, here]
             for step in range(1, lon_count):
-                rs_copy(turn, step).wait_recv()
-                summed = summed + part_in[turn, step - 1]
-            coef[turn, pl.ds(lon * per, per), :, :KMAX] = summed[:, :, :KMAX] * keep
-            coef[turn, pl.ds(lon * per, per), :, KMAX:] = summed[:, :, KMAX:] * keep
-            for step in range(1, lon_count):
-                ag_copy(turn, step).start()
-            for step in range(1, lon_count):
-                rs_copy(turn, step).wait_send()
-            for step in range(1, lon_count):
-                ag_arrival(turn, step).wait_recv()
-            for step in range(1, lon_count):
-                ag_copy(turn, step).wait_send()
-            sums = coef[turn].reshape(levels * rows, 2 * KMAX)
-            real = sums[:, :KMAX]
-            imag = sums[:, KMAX:]
+                summed = summed + part_in[turn, lax.rem(lon + step, lon_count), here]
+            real = (summed[:, :, :KMAX] * keep).reshape(per * rows, KMAX)
+            imag = (summed[:, :, KMAX:] * keep).reshape(per * rows, KMAX)
             return jnp.concatenate(
                 [real * cosine + imag * sine, imag * cosine - real * sine], axis=1)
 
-        for level in range(levels):
-            tend[level, :, :cols] = stencil(0, level)
-        local = filtered_coefficients(0)
-        filtered = dot3(local, syn)
-        q[...] = q[...] + filtered.reshape(levels, rows, width)
+        def sums_sent(turn):
+            for piece in range(PIECES):
+                for step in range(1, lon_count):
+                    sum_copy(turn, piece, lax.rem(lon + step, lon_count)).wait_send()
+
+        for piece in range(PIECES):
+            analyse(0, piece)
+        pole_rows = []
+        for piece in range(PIECES):
+            here = slice(piece * per, (piece + 1) * per)
+            local = collect(0, piece)
+            q[here] = q[here] + dot3(local, syn).reshape(per, rows, width)
+            local = local.reshape(per, rows, 2 * KMAX)
+            pole_rows.append(jnp.where(first, local[:, 0, :], local[:, rows - 1, :]))
         pack_rows(1)
 
         @pl.when(jnp.logical_not(last))
@@ -330,8 +337,7 @@
         def _():
             row_copy(1, 1).start()
 
-        by_level = local.reshape(levels, rows, 2 * KMAX)
-        pole_row = jnp.where(first, by_level[:, 0, :], by_level[:, rows - 1, :]) * parity
+        pole_row = jnp.concatenate(pole_rows, axis=0) * parity
         pole_sum = pole_in[...] + dot3(pole_row, syn)
 
         @pl.when(last)
@@ -352,16 +358,15 @@
             row_copy(1, 0).wait_recv()
             row_copy(1, 1).wait_send()
 
-        for level in range(levels):
-            tend[level, :, :cols] = stencil(1, level)
-        filtered = dot3(filtered_coefficients(1), syn)
-        filtered = filtered.reshape(levels, rows, width)
-        for level in range(levels):
-            out[level] = q[level, :, :cols] + filtered[level, :, :cols]
-
-    store = pltpu.make_async_copy(out, out_hbm, load_sem.at[0])
-    store.start()
-    store.wait()
+        for piece in range(PIECES):
+            analyse(1, piece)
+        for piece in range(PIECES):
+            filtered = dot3(collect(1, piece), syn).reshape(per, rows, width)
+            for level in range(per):
+                there = piece * per + level
+                out[there] = q[there, :, :cols] + filtered[level, :, :cols]
+        sums_sent(0)
+        sums_sent(1)
 
 
 def shards(tracer, zonal_courant, north_courant, cutoff):
@@ -370,16 +375,14 @@
     lon_count = lax.axis_size("lon")
     cap_blocks = lat_count // 8
     width = -(-(cols + 2) // LANES) * LANES
-    per = levels // lon_count
     analysis, synthesis, phase = tables(cols, width, lon_count)
-    peers = lon_count - 1
     dma = pltpu.SemaphoreType.DMA
     anywhere = pl.BlockSpec(memory_space=pl.ANY)
     return pl.pallas_call(
         functools.partial(kernel, lat_count, lon_count, cap_blocks),
-        out_shape=jax.ShapeDtypeStruct(tracer.shape, F32),
+        out_shape=pltpu.VMEM(tracer.shape, F32),
         in_specs=[pl.BlockSpec(memory_space=pltpu.SMEM)] + [anywhere] * 6,
-        out_specs=anywhere,
+        out_specs=pl.BlockSpec(memory_space=pltpu.VMEM),
         scratch_shapes=[
             pltpu.VMEM((levels, rows, cols), F32),
             pltpu.VMEM((levels, rows, cols), F32),
@@ -387,7 +390,6 @@
             pltpu.VMEM(analysis.shape, BF16),
             pltpu.VMEM(synthesis.shape, BF16),
             pltpu.VMEM(phase.shape[1:], F32),
-            pltpu.VMEM((levels, rows, cols), F32),
             pltpu.VMEM((levels, rows, width), F32),
             pltpu.VMEM((levels, rows, width), F32),
             pltpu.VMEM((2, 2, levels, width), F32),
@@ -396,12 +398,11 @@
             pltpu.VMEM((2, 2, rows, LANES), F32),
             pltpu.VMEM((levels, width), F32),
             pltpu.VMEM((2, levels, rows, 2 * KMAX), F32),
-            pltpu.VMEM((2, peers, per, rows, 2 * KMAX), F32),
-            pltpu.VMEM((2, levels, rows, 2 * KMAX), F32),
+            pltpu.VMEM((2, lon_count, levels, rows, 2 * KMAX), F32),
             dma((6,)),
             dma((2, 2)), dma((2, 2)), dma((2, 2)), dma((2, 2)),
             dma(()), dma(()),
-            dma((2, peers)), dma((2, peers)), dma((2, peers)), dma((2, peers)),
+            dma((2, PIECES, lon_count)), dma((2, PIECES, lon_count)),
         ],
         compiler_params=pltpu.CompilerParams(collective_id=0, has_side_effects=True),
     )(cutoff, tracer, zonal_courant, north_courant,

time: 32.2 us -> 28.4 us (0.88)
  Pallas kernels: 30.3 us -> 27.5 us
  local copies, waits for them, and re-layouts: 1.77 us -> 0.75 us
    pallas_call x1, Pallas kernels: 30.3 us -> 27.5 us  [shards(): pl.pallas_call(functools.partial(kernel, lat_count, lon_count, cap_blocks...]
    unnamed x1, local copies, waits for them, and re-layouts: 1.77 us -> 0.75 us
where the time goes in v2:
time: 28.4 us; the launch traced here: 28.2 us
  Pallas kernels  27.5 us (97%)
  local copies, waits for them, and re-layouts  0.75 us (3%)
    pallas_call x1, Pallas kernels, shards(): pl.pallas_call(functools.partial(kernel, lat_count, lon_count, cap_blocks...  27.5 us
    unnamed x1, local copies, waits for them, and re-layouts  0.75 us

profile of v2, /device:TPU:0, one launch (start us, length us, event | category | flops | bytes accessed | tf_op | source)
XLA Modules:
  0.0 28.2 jit_solution(7803244526060627221)
XLA Ops:
  0.0 27.5 %shard_map.73 = f32[16,8,720]{2,1,0:T(8,128)S(1)} custom-call(s32[16]{0:T(128)} %cut_ref.1, f32[16,8,720]{2,1,0:T(8,128)} %tracer.1, f32[16,8,720]{2,1,0:T(8,128)} %zonal.1, f32[16,8,720]{2,1,0:T(8,128)} %north.1, bf16[2,768,256]{2,1,0:T(8,128)(2,1)} %constant.6.clone.ana_hbm, bf16[2,256,768]{2,1,0:T(8,128)(2,1)} %constant.7.clone.syn_hbm, ...), custom_call_target="tpu_custom_call" | custom-call | tf_op jit(solution)/shard_map/pallas_call | solution.py:381
  27.5 0.7 %copy.9 = f32[16,8,720]{2,1,0:T(8,128)} copy(f32[16,8,720]{2,1,0:T(8,128)S(1)} %shard_map.73) | data formatting | bytes 737280

commit v3 on v0

v3 whole, which is shorter than its diff:
```python
import functools
import math

import jax
import jax.numpy as jnp
import numpy as np
from jax import lax
from jax.experimental import pallas as pl
from jax.experimental.pallas import tpu as pltpu
from jax.sharding import PartitionSpec as P

KMAX = 128
DIFFUSION = 0.2
LANES = 128
MESH = pl.DeviceIdType.MESH
F32 = jnp.float32
BF16 = jnp.bfloat16


def split_table(table):
    high = table.astype(np.float32).astype(BF16)
    low = (table - high.astype(np.float64)).astype(np.float32).astype(BF16)
    return np.stack([high, low])


def trig(columns, total):
    modes = np.arange(KMAX)
    angle = (columns[:, None] * modes[None, :] % total) * (2.0 * math.pi / total)
    return np.concatenate([np.cos(angle), np.sin(angle)], axis=1)


def tables(cols, width, lon_count):
    lane = np.arange(width)
    lane = np.where(lane == width - 1, -1, lane)
    total = cols * lon_count
    both = trig(lane, total)
    ends = np.zeros((lon_count, 8, 2 * KMAX), np.float32)
    ends[:, 0] = trig(np.arange(lon_count) * cols, total)
    ends[:, 1] = trig(np.arange(lon_count) * cols + cols - 1, total)
    return split_table(both), split_table(both.T.copy()), ends


def split(value):
    high = value.astype(BF16)
    low = (value - high.astype(F32)).astype(BF16)
    return high, low


def dot3(value, table):
    high, low = split(value)
    t_high = table[0]
    t_low = table[1]
    dot = functools.partial(jnp.dot, preferred_element_type=F32)
    return dot(high, t_high) + (dot(low, t_high) + dot(high, t_low))


def kernel(
    lat_count, lon_count, cap_blocks,
    cut_ref, tracer, zonal, north, ana_hbm, syn_hbm, ends_hbm, out,
    q_in, zc, nc, ana, syn, ends, q, tend,
    row_first, row_second, col_out, col_in, part, part_in, extra,
    load_sem, row_send, row_recv, col_send, col_recv, sum_send, sum_recv,
):
    rows, levels, cols = q_in.shape
    width = q.shape[2]
    total = cols * lon_count
    lat = lax.axis_index("lat")
    lon = lax.axis_index("lon")
    polar = jnp.logical_or(lat < cap_blocks, lat >= lat_count - cap_blocks)
    first = lat == 0
    last = lat == lat_count - 1
    east = lax.rem(lon + 1, lon_count)
    west = lax.rem(lon + lon_count - 1, lon_count)
    across = lax.rem(lon + lon_count // 2, lon_count)
    peers = [lax.rem(lon + step, lon_count) for step in range(1, lon_count)]
    order = [0, rows - 1, 1, rows - 2] + list(range(2, rows - 2))
    pieces = (((2, rows), (0, 2)), ((4, rows), (0, 4)))

    loads = []
    for index, (source, target) in enumerate(((tracer, q_in), (zonal, zc), (north, nc))):
        for row in range(rows):
            loads.append(pltpu.make_async_copy(
                source.at[:, row, :], target.at[row], load_sem.at[index * rows + row]))
    for load in loads[:rows]:
        load.start()

    barrier = pltpu.get_barrier_semaphore()

    def greet(there):
        pl.semaphore_signal(barrier, inc=1, device_id=there, device_id_type=MESH)

    @pl.when(jnp.logical_not(first))
    def _():
        greet({"lat": lat - 1, "lon": lon})

    @pl.when(jnp.logical_not(last))
    def _():
        greet({"lat": lat + 1, "lon": lon})

    @pl.when(polar)
    def _():
        for peer in peers:
            greet({"lat": lat, "lon": peer})

    @pl.when(jnp.logical_not(polar))
    def _():
        greet({"lat": lat, "lon": east})
        greet({"lat": lat, "lon": west})

    for load in loads[rows:]:
        load.start()
    tables_in = [
        pltpu.make_async_copy(ana_hbm, ana, load_sem.at[3 * rows]),
        pltpu.make_async_copy(syn_hbm, syn, load_sem.at[3 * rows + 1]),
        pltpu.make_async_copy(ends_hbm, ends, load_sem.at[3 * rows + 2]),
    ]
    for load in tables_in:
        load.start()

    edge = first.astype(jnp.int32) + last.astype(jnp.int32)
    sides = jnp.where(polar, lon_count - 1, 2)
    pl.semaphore_wait(barrier, 2 - edge + sides)

    def row_copy(turn, slot, row, there):
        source = tracer.at[:, row, :] if turn == 0 else q.at[row]
        target = row_first if turn == 0 else row_second
        return pltpu.make_async_remote_copy(
            source, target.at[slot],
            row_send.at[turn, 0 if row else 1], row_recv.at[turn, slot],
            device_id=there, device_id_type=MESH)

    def to_north(turn):
        return row_copy(turn, 0, rows - 1, {"lat": lat + 1, "lon": lon})

    def to_south(turn):
        return row_copy(turn, 1, 0, {"lat": lat - 1, "lon": lon})

    def over_north():
        return row_copy(0, 1, rows - 1, {"lat": lat, "lon": across})

    def over_south():
        return row_copy(0, 0, 0, {"lat": lat, "lon": across})

    @pl.when(last)
    def _():
        over_north().start()

    @pl.when(first)
    def _():
        over_south().start()

    @pl.when(jnp.logical_not(last))
    def _():
        to_north(0).start()

    @pl.when(jnp.logical_not(first))
    def _():
        to_south(0).start()

    def rows_arrive(turn):
        @pl.when(jnp.logical_not(last))
        def _():
            to_south(turn).wait_recv()
            to_north(turn).wait_send()

        @pl.when(jnp.logical_not(first))
        def _():
            to_north(turn).wait_recv()
            to_south(turn).wait_send()

    def poles_arrive():
        @pl.when(last)
        def _():
            over_north().wait()

        @pl.when(first)
        def _():
            over_south().wait()

    lane = lax.broadcasted_iota(jnp.int32, (levels, LANES), 1)
    end_tile = (cols - 1) // LANES * LANES
    end_lane = (cols - 1) % LANES
    east_tile = cols // LANES * LANES
    west_tile = width - LANES

    def pack_cols(turn):
        packed = jnp.zeros((levels, LANES), F32)

        def put(packed, at, tile, came_from):
            return jnp.where(lane == at, pltpu.roll(tile, (at - came_from) % LANES, 1), packed)

        for row in range(rows):
            packed = put(packed, row, q[row, :, end_tile:end_tile + LANES], end_lane)
            packed = put(packed, rows + row, q[row, :, 0:LANES], 0)
        return packed

    def pack_factors(packed):
        for row in range(rows):
            tile = zc[row, :, end_tile:cols]
            if cols - end_tile < LANES:
                tile = jnp.concatenate(
                    [tile, jnp.zeros((levels, LANES - cols + end_tile), F32)], axis=1)
            factor = DIFFUSION - 0.5 * tile
            packed = jnp.where(
                lane == 2 * rows + row,
                pltpu.roll(factor, (2 * rows + row - end_lane) % LANES, 1), packed)
            factor = DIFFUSION + 0.5 * zc[row, :, 0:LANES]
            packed = jnp.where(
                lane == 3 * rows + row, pltpu.roll(factor, 3 * rows + row, 1), packed)
        return packed

    def place_cols(turn):
        from_west = col_in[turn, west]
        from_east = col_in[turn, east]
        for row in range(rows):
            tile = q[row, :, east_tile:east_tile + LANES]
            moved = pltpu.roll(from_east, (cols % LANES - rows - row) % LANES, 1)
            q[row, :, east_tile:east_tile + LANES] = jnp.where(lane == cols % LANES, moved, tile)
            tile = q[row, :, west_tile:west_tile + LANES]
            moved = pltpu.roll(from_west, (LANES - 1 - row) % LANES, 1)
            q[row, :, west_tile:west_tile + LANES] = jnp.where(lane == LANES - 1, moved, tile)

    def col_copy(turn, target):
        return pltpu.make_async_remote_copy(
            col_out.at[turn], col_in.at[turn, lon],
            col_send.at[turn, target], col_recv.at[turn, lon],
            device_id={"lat": lat, "lon": target}, device_id_type=MESH)

    def col_arrival(turn, source):
        theirs = col_in.at[turn, source]
        return pltpu.make_async_remote_copy(
            theirs, theirs, col_send.at[turn, source], col_recv.at[turn, source],
            device_id={"lat": lat, "lon": source}, device_id_type=MESH)

    def sum_copy(turn, piece, target):
        low, high = pieces[turn][piece]
        return pltpu.make_async_remote_copy(
            part.at[turn, low:high], part_in.at[turn, lon, low:high],
            sum_send.at[turn, piece, target], sum_recv.at[turn, piece, lon],
            device_id={"lat": lat, "lon": target}, device_id_type=MESH)

    def sum_arrival(turn, piece, source):
        low, high = pieces[turn][piece]
        theirs = part_in.at[turn, source, low:high]
        return pltpu.make_async_remote_copy(
            theirs, theirs, sum_send.at[turn, piece, source], sum_recv.at[turn, piece, source],
            device_id={"lat": lat, "lon": source}, device_id_type=MESH)

    def farthest_first(send):
        for distance in range(lon_count - 1, 0, -1):
            @pl.when(lon + distance < lon_count)
            def _():
                send(lon + distance)

            @pl.when(lon - distance >= 0)
            def _():
                send(lon - distance)

    def stencil(turn, row):
        beyond = row_first if turn == 0 else row_second
        here = q[row]
        to_east = pltpu.roll(here, width - 1, 1)[:, :cols]
        to_west = pltpu.roll(here, 1, 1)[:, :cols]
        here = here[:, :cols]
        up = q[row + 1, :, :cols] if row < rows - 1 else beyond[1, :, :cols]
        down = q[row - 1, :, :cols] if row else beyond[0, :, :cols]
        return (-0.5 * zc[row] * (to_east - to_west)
                - 0.5 * nc[row] * (up - down)
                + DIFFUSION * (to_east + to_west + up + down - 4.0 * here))

    q[:, :, (width - LANES):] = jnp.zeros((rows, levels, LANES), F32)
    for load in loads[:rows]:
        load.wait()
    for row in range(rows):
        q[row, :, :cols] = q_in[row]

    @pl.when(jnp.logical_not(polar))
    def _():
        col_out[0] = pack_cols(0)
        for side in (east, west):
            col_copy(0, side).start()
        for load in loads[rows:] + tables_in:
            load.wait()
        for side in (east, west):
            col_arrival(0, side).wait_recv()
        place_cols(0)
        rows_arrive(0)
        for row in range(rows):
            tend[row, :, :cols] = stencil(0, row)
        for row in range(rows):
            q[row, :, :cols] = q[row, :, :cols] + tend[row, :, :cols]
        to_north(1).start()
        to_south(1).start()
        col_out[1] = pack_cols(1)
        for side in (east, west):
            col_copy(1, side).start()
        for side in (east, west):
            col_arrival(1, side).wait_recv()
        rows_arrive(1)
        place_cols(1)
        for row in range(rows):
            out[:, row, :] = q[row, :, :cols] + stencil(1, row)
        for turn in range(2):
            for side in (east, west):
                col_copy(turn, side).wait_send()

    @pl.when(polar)
    def _():
        tend[:, :, (width - LANES):] = jnp.zeros((rows, levels, LANES), F32)
        for load in loads[rows:2 * rows]:
            load.wait()
        col_out[0] = pack_factors(pack_cols(0))
        farthest_first(lambda target: col_copy(0, target).start())
        for load in loads[2 * rows:] + tables_in:
            load.wait()

        cosine = ends[lon, 0:1, :KMAX]
        sine = ends[lon, 0:1, KMAX:]
        offset = jnp.where(
            lat < cap_blocks, lat * rows, (lat - lat_count + 2 * cap_blocks) * rows)
        mode = lax.broadcasted_iota(jnp.int32, (1, KMAX), 1)
        weight = jnp.where(mode == 0, 1.0 / total, 2.0 / total).astype(F32)
        keep = [jnp.where(mode < cut_ref[offset + row], weight, 0.0) for row in range(rows)]
        parity = 1.0 - 2.0 * (lax.broadcasted_iota(jnp.int32, (1, 2 * KMAX), 1) % 2).astype(F32)

        def analyse(turn, piece):
            low, high = pieces[turn][piece]
            count = high - low
            for slot in range(low, high):
                tend[slot, :, :cols] = stencil(turn, order[slot])
            partial = dot3(tend[low:high].reshape(count * levels, width), ana)
            real = partial[:, :KMAX]
            imag = partial[:, KMAX:]
            part[turn, low:high, :, :KMAX] = (real * cosine - imag * sine).reshape(count, levels, KMAX)
            part[turn, low:high, :, KMAX:] = (real * sine + imag * cosine).reshape(count, levels, KMAX)
            farthest_first(lambda target: sum_copy(turn, piece, target).start())

        def collect(turn, piece):
            low, high = pieces[turn][piece]
            for peer in peers:
                sum_arrival(turn, piece, peer).wait_recv()
            result = []
            for slot in range(low, high):
                summed = part[turn, slot]
                if turn == 0:
                    summed = summed + extra[slot]
                for peer in peers:
                    summed = summed + part_in[turn, peer, slot]
                real = summed[:, :KMAX] * keep[order[slot]]
                imag = summed[:, KMAX:] * keep[order[slot]]
                result.append(jnp.concatenate(
                    [real * cosine + imag * sine, imag * cosine - real * sine], axis=1))
            return result

        def synthesise(parts):
            return dot3(jnp.concatenate(parts, axis=0), syn).reshape(len(parts), levels, width)

        analyse(0, 0)
        rows_arrive(0)
        poles_arrive()
        analyse(0, 1)

        for peer in peers:
            col_arrival(0, peer).wait_recv()
        col_in[0, lon] = col_out[0]
        place_cols(0)
        packed = [col_in[0, place] for place in range(lon_count)]
        added = [jnp.zeros((levels, 2 * KMAX), F32) for _ in range(rows)]
        for place in range(lon_count):
            behind = packed[place - 1]
            ahead = packed[(place + 1) % lon_count]
            at_last = packed[place] * pltpu.roll(ahead, rows, 1)
            at_first = packed[place] * pltpu.roll(behind, 3 * rows, 1)
            for row in range(rows):
                column = at_last[:, 2 * rows + row:2 * rows + row + 1]
                added[row] = added[row] + column * ends[place, 1:2, :]
                column = at_first[:, 3 * rows + row:3 * rows + row + 1]
                added[row] = added[row] + column * ends[place, 0:1, :]
        for slot in range(rows):
            extra[slot] = added[order[slot]]

        low, high = pieces[0][0]
        filtered = synthesise(collect(0, 0))
        for slot in range(low, high):
            q[order[slot]] = q[order[slot]] + filtered[slot - low]
        analyse(1, 0)

        local = collect(0, 1)
        pole_row = jnp.where(first, local[0], local[1]) * parity
        filtered = synthesise(local + [pole_row])
        q[0] = q[0] + filtered[0]
        q[rows - 1] = q[rows - 1] + filtered[1]

        @pl.when(jnp.logical_not(last))
        def _():
            to_north(1).start()

        @pl.when(jnp.logical_not(first))
        def _():
            to_south(1).start()

        @pl.when(last)
        def _():
            row_second[1, :, :cols] = row_first[1] + filtered[2, :, :cols]

        @pl.when(first)
        def _():
            row_second[0, :, :cols] = row_first[0] + filtered[2, :, :cols]

        rows_arrive(1)
        analyse(1, 1)
        for piece in range(2):
            low, high = pieces[1][piece]
            filtered = synthesise(collect(1, piece))
            for slot in range(low, high):
                row = order[slot]
                out[:, row, :] = q[row, :, :cols] + filtered[slot - low, :, :cols]
        for peer in peers:
            col_copy(0, peer).wait_send()
            for turn in range(2):
                for piece in range(2):
                    sum_copy(turn, piece, peer).wait_send()


def shards(tracer, zonal_courant, north_courant, cutoff):
    levels, rows, cols = tracer.shape
    lat_count = lax.axis_size("lat")
    lon_count = lax.axis_size("lon")
    cap_blocks = lat_count // 8
    width = -(-(cols + 2) // LANES) * LANES
    analysis, synthesis, ends = tables(cols, width, lon_count)
    dma = pltpu.SemaphoreType.DMA
    anywhere = pl.BlockSpec(memory_space=pl.ANY)
    return pl.pallas_call(
        functools.partial(kernel, lat_count, lon_count, cap_blocks),
        out_shape=pltpu.VMEM(tracer.shape, F32),
        in_specs=[pl.BlockSpec(memory_space=pltpu.SMEM)] + [anywhere] * 6,
        out_specs=pl.BlockSpec(memory_space=pltpu.VMEM),
        scratch_shapes=[
            pltpu.VMEM((rows, levels, cols), F32),
            pltpu.VMEM((rows, levels, cols), F32),
            pltpu.VMEM((rows, levels, cols), F32),
            pltpu.VMEM(analysis.shape, BF16),
            pltpu.VMEM(synthesis.shape, BF16),
            pltpu.VMEM(ends.shape, F32),
            pltpu.VMEM((rows, levels, width), F32),
            pltpu.VMEM((rows, levels, width), F32),
            pltpu.VMEM((2, levels, cols), F32),
            pltpu.VMEM((2, levels, width), F32),
            pltpu.VMEM((2, levels, LANES), F32),
            pltpu.VMEM((2, lon_count, levels, LANES), F32),
            pltpu.VMEM((2, rows, levels, 2 * KMAX), F32),
            pltpu.VMEM((2, lon_count, rows, levels, 2 * KMAX), F32),
            pltpu.VMEM((rows, levels, 2 * KMAX), F32),
            dma((3 * rows + 3,)),
            dma((2, 2)), dma((2, 2)), dma((2, lon_count)), dma((2, lon_count)),
            dma((2, 2, lon_count)), dma((2, 2, lon_count)),
        ],
        compiler_params=pltpu.CompilerParams(collective_id=0, has_side_effects=True),
    )(cutoff, tracer, zonal_courant, north_courant,
      jnp.asarray(analysis), jnp.asarray(synthesis), jnp.asarray(ends))


def solution(mesh):
    return jax.shard_map(
        shards,
        mesh=mesh,
        in_specs=(P(None, "lat", "lon"), P(None, "lat", "lon"), P(None, "lat", "lon"), P()),
        out_specs=P(None, "lat", "lon"),
        check_vma=False,
    )
```

time: 136 us -> 24.8 us (0.18)
  waiting for transfers between devices: 86.4 us -> 0 us
  Pallas kernels: 0 us -> 23.9 us
  starting transfers between devices: 22.5 us -> 0 us
  between operations: 13.6 us -> 0.01 us
  matrix products: 6.6 us -> 0 us
  other arithmetic: 4.59 us -> 0 us
  local copies, waits for them, and re-layouts: 2.6 us -> 0.75 us
    psum x2 -> x0, waiting for transfers between devices: 73.7 us -> none  [shards(): coefficients = lax.psum(partial_coeffs, 'lon')]
    pallas_call x0 -> x1, Pallas kernels: none -> 23.9 us  [shards(): pl.pallas_call(functools.partial(kernel, lat_count, lon_count, cap_blocks...]
    ppermute x10 -> x0, starting transfers between devices: 22.5 us -> none  [the longest x4 8.73 us: with_halo(): lax.ppermute(lax.slice_in_dim(block, 0, width, axis=dim), axis, backward)]
    ppermute x10 -> x0, waiting for transfers between devices: 12.7 us -> none  [the longest x4 7.37 us: with_halo(): lax.ppermute(lax.slice_in_dim(block, block.shape[dim] - width, None, axis...]
    dot_general x4 -> x0, matrix products: 6.6 us -> none  [the longest x2 4.25 us: shards(): filtered = jnp.dot(coefficients, synthesis, precision=lax.Precision.HIGHEST)]
    add x3 -> x0, other arithmetic: 2.19 us -> none  [the longest x2 2.18 us: shards(): -0.5 * zonal_courant * (east_cell - west_cell)]
    mul x1 -> x0, other arithmetic: 1.62 us -> none  [fourier_tables(): cosine * weights[None, :]]
  transfers between devices with their start and end apart: 12 -> 0, of which waited for: 8 -> 0; matrix products, arithmetic and copies ran while one was open for 1% -> 0% of each run, Pallas kernels for 0% -> 0%
where the time goes in v3:
time: 24.8 us; the launch traced here: 24.7 us
  Pallas kernels  23.9 us (96%)
  local copies, waits for them, and re-layouts  0.75 us (3%)
    pallas_call x1, Pallas kernels, shards(): pl.pallas_call(functools.partial(kernel, lat_count, lon_count, cap_blocks...  23.9 us
    unnamed x1, local copies, waits for them, and re-layouts  0.75 us

profile of v3, /device:TPU:0, one launch (start us, length us, event | category | flops | bytes accessed | tf_op | source)
XLA Modules:
  0.0 24.7 jit_solution(3581891203686026017)
XLA Ops:
  0.0 23.9 %shard_map.73 = f32[16,8,720]{2,1,0:T(8,128)S(1)} custom-call(s32[16]{0:T(128)} %cut_ref.1, f32[16,8,720]{2,1,0:T(8,128)} %tracer.1, f32[16,8,720]{2,1,0:T(8,128)} %zonal.1, f32[16,8,720]{2,1,0:T(8,128)} %north.1, bf16[2,768,256]{2,1,0:T(8,128)(2,1)} %constant.6.clone.ana_hbm, bf16[2,256,768]{2,1,0:T(8,128)(2,1)} %constant.7.clone.syn_hbm, ...), custom_call_target="tpu_custom_call" | custom-call | tf_op jit(solution)/shard_map/pallas_call | solution.py:434
  23.9 0.7 %copy.9 = f32[16,8,720]{2,1,0:T(8,128)} copy(f32[16,8,720]{2,1,0:T(8,128)S(1)} %shard_map.73) | data formatting | bytes 737280
